TPU v7x, 512 devices: a whole 4x4x16 slice. The times are simulated.
512 devices in a mesh: grid: 4 (over z_lo), gx: 16 (over x, y), gy: 8 (over z_hi, core).
Axes of the slice: x: 4, y: 4, z: 16 (z_hi: 4, z_lo: 4; z = z_hi * 4 + z_lo), core: 2. Of those that a mesh axis runs over, the one named last changes fastest.
Arguments:
- adjoint: float32 [4, 24, 512, 2048], P('grid', None, 'gx', 'gy'), may hold values from -6 to 6
- sea_mask: int32 [4, 512, 2048], P('grid', 'gx', 'gy'), may hold values 0 or 1
- diffusivity: float32 [4, 512, 2048], P('grid', 'gx', 'gy'), may hold values from 0.03 to 0.24
- aggregation: float32 [4, 512, 2048], P('grid', 'gx', 'gy'), may hold values from 0.02 to 0.3
- breakup: float32 [4, 512, 2048], P('grid', 'gx', 'gy'), may hold values from 0.02 to 0.3
- sponge: float32 [4, 512, 2048], P('grid', 'gx', 'gy'), may hold values from 0.05 to 0.6
- settling: float32 [4, 3], replicated, may hold values from 0.05 to 0.5
- partner_flip: int32 [3, 16, 8], replicated, may hold values from 0 to 1
- row_offset: int32 [3, 16, 8], replicated, may hold values from 0 to 16
- col_offset: int32 [3, 16, 8], replicated, may hold values from 0 to 128
Outputs:
- adjoint_out: float32 [4, 24, 512, 2048], P('grid', None, 'gx', 'gy')
Inputs may be any that keep to these rules, and one draw needn't show every extreme that they name: `partner_flip`: every child tile is paired with exactly one parent tile in its own tile column, in its own tile row or the row whose index differs in the lowest bit; a parent tile serves 0 to 6 child tiles. `row_offset`: the footprint lies inside the paired parent tile. `col_offset`: the footprint lies inside the paired parent tile.
All inputs are finite; a program needn't handle non-finite values. No bound on the sum of `sea_mask` on one device may be relied on, other than what follows from the above.
Results may differ from a plain program's by a relative error of at most 0.0001.
Values sent between devices are 32-bit elements; how exact they have to be, the bound alone decides.
A program may use at most 64 MiB of HBM per device.

v0:
```python
import jax
import jax.numpy as jnp
from jax import lax
from jax.sharding import PartitionSpec as P

NCLS = 3
LEV = 8
STEPS = 2
relaxation = 0.125


def partner(value, axis, distance):
    mask = 2**distance
    pairs = [(source, source ^ mask) for source in range(lax.axis_size(axis))]
    return lax.ppermute(value, axis, pairs)


def spread(block, axis, holder):
    block = jnp.where(lax.axis_index(axis) == holder, block, jnp.zeros_like(block))
    return lax.psum(block, axis)


def padded_2(shard, sides, width):
    for axis, dim in sides:
        size, length = (lax.axis_size(axis), shard.shape[dim])
        up = [(i, (i + 1) % size) for i in range(size - 1)]
        down = [(j, i) for i, j in up]
        last = lax.slice_in_dim(shard, length - width, length, axis=dim)
        leading = lax.slice_in_dim(shard, 0, width, axis=dim)
        before = lax.ppermute(last, axis, up)
        after = lax.ppermute(leading, axis, down)
        shard = jnp.concatenate([before, shard, after], axis=dim)
    return shard


def block_sums(values):
    shape = values.shape
    return values.reshape(shape[:-2] + (shape[-2] // 2, 2, shape[-1] // 2, 2)).sum(axis=(-3, -1))


def expand_cells(values):
    return jnp.repeat(jnp.repeat(values, 2, axis=-2), 2, axis=-1)


def floc_adjoint(values, aggregation, breakup):
    shape = values.shape
    split = values.reshape((shape[0], NCLS, LEV) + shape[2:])
    agg = aggregation[:, None]
    brk = breakup[:, None]
    first = split[:, 0]
    second = split[:, 1]
    third = split[:, 2]
    new_first = (1.0 - agg) * first + agg * second
    new_second = brk * first + (1.0 - agg - brk) * second + agg * third
    new_third = brk * second + (1.0 - brk) * third
    return jnp.stack([new_first, new_second, new_third], axis=1).reshape(shape)


def settle_adjoint(values, rates):
    shape = values.shape
    split = values.reshape((shape[0], NCLS, LEV) + shape[2:])
    below = jnp.concatenate([split[:, :, 1:], jnp.zeros_like(split[:, :, :1])], axis=2)
    speed = rates[:, :, None, None, None]
    return ((1.0 - speed) * split + speed * below).reshape(shape)


def local(
    adjoint,
    sea_mask,
    diffusivity,
    aggregation,
    breakup,
    sponge,
    settling,
    partner_flip,
    row_offset,
    col_offset,
):
    n_grid = lax.axis_size("grid")
    slots = n_grid - 1
    grid_index = lax.axis_index("grid")
    row_index = lax.axis_index("gx")
    col_index = lax.axis_index("gy")
    partner_row = jnp.bitwise_xor(row_index, 1)
    is_parent = grid_index == 0
    own_slot = jnp.maximum(grid_index - 1, 0)
    flips_here = partner_flip[:, row_index, col_index]
    flips_there = partner_flip[:, partner_row, col_index]
    tops_here = row_offset[:, row_index, col_index]
    lefts_here = col_offset[:, row_index, col_index]
    tops_there = row_offset[:, partner_row, col_index]
    lefts_there = col_offset[:, partner_row, col_index]
    keep_here = (flips_here == 0).astype(jnp.float32)
    take_there = (flips_there == 1).astype(jnp.float32)
    components = adjoint.shape[1]
    cells_r = adjoint.shape[2]
    cells_c = adjoint.shape[3]
    half_r = cells_r // 2
    half_c = cells_c // 2
    anchor = jnp.zeros((), jnp.int32)
    settle_rates = settling[grid_index][None]
    weights = sponge[0]
    wet_mask = sea_mask.astype(jnp.float32)[:, None]
    row_ids = lax.broadcasted_iota(jnp.int32, (cells_r, cells_c), 0)
    col_ids = lax.broadcasted_iota(jnp.int32, (cells_r, cells_c), 1)
    covered = jnp.zeros((cells_r, cells_c), jnp.float32)
    for slot in range(slots):
        for tops, lefts, flags in (
            (tops_here, lefts_here, keep_here),
            (tops_there, lefts_there, take_there),
        ):
            inside = (
                (row_ids >= tops[slot])
                & (row_ids < tops[slot] + half_r)
                & (col_ids >= lefts[slot])
                & (col_ids < lefts[slot] + half_c)
            )
            covered = covered + flags[slot] * inside.astype(jnp.float32)
    state = adjoint
    for step_number in range(STEPS):
        current = state[0]
        child_block = block_sums(weights * current)
        down_here = jnp.stack(
            [
                keep_here[slot]
                * lax.dynamic_slice(
                    current,
                    (anchor, tops_here[slot], lefts_here[slot]),
                    (components, half_r, half_c),
                )
                for slot in range(slots)
            ]
        )
        down_there = jnp.stack(
            [
                take_there[slot]
                * lax.dynamic_slice(
                    current,
                    (anchor, tops_there[slot], lefts_there[slot]),
                    (components, half_r, half_c),
                )
                for slot in range(slots)
            ]
        )
        gathered_up = lax.all_gather(child_block[None], "grid", axis=0, tiled=True)[1:]
        up_keep = keep_here[:, None, None, None] * gathered_up
        up_send = (1.0 - keep_here)[:, None, None, None] * gathered_up
        up_cross, down_cross = partner((up_send, down_there), "gx", 0)
        down_all = spread(down_here + down_cross, "grid", 0)
        from_parent = down_all[own_slot]
        child_new = (1.0 - weights) * current + relaxation / 4.0 * expand_cells(from_parent)
        gathered = jnp.zeros_like(current)
        for slot in range(slots):
            for tops, lefts, pieces in (
                (tops_here, lefts_here, up_keep),
                (tops_there, lefts_there, up_cross),
            ):
                existing = lax.dynamic_slice(
                    gathered, (anchor, tops[slot], lefts[slot]), (components, half_r, half_c)
                )
                gathered = lax.dynamic_update_slice(
                    gathered, existing + pieces[slot], (anchor, tops[slot], lefts[slot])
                )
        parent_new = (1.0 - relaxation * covered) * current + gathered
        state = jnp.where(is_parent, parent_new, child_new)[None]
        state = floc_adjoint(state, aggregation, breakup)
        state = settle_adjoint(state, settle_rates)
        wet = wet_mask * state
        flux = diffusivity[:, None] * wet
        padded = padded_2(flux, (("gx", 2), ("gy", 3)), 1)
        state = (
            wet
            + padded[:, :, :-2, 1:-1]
            + padded[:, :, 2:, 1:-1]
            + padded[:, :, 1:-1, :-2]
            + padded[:, :, 1:-1, 2:]
            - 4.0 * flux
        )
    return state


def solution(mesh):
    in_specs = (
        P("grid", None, "gx", "gy"),
        P("grid", "gx", "gy"),
        P("grid", "gx", "gy"),
        P("grid", "gx", "gy"),
        P("grid", "gx", "gy"),
        P("grid", "gx", "gy"),
        P(),
        P(),
        P(),
        P(),
    )
    out_specs = P("grid", None, "gx", "gy")
    return jax.shard_map(local, mesh=mesh, in_specs=in_specs, out_specs=out_specs, check_vma=False)
```

profile of v0, /device:TPU:25, one launch (start us, length us, event | category | flops | bytes accessed | tf_op | source)
XLA Modules:
  0.0 421.5 jit_solution(10322343063372970234)
XLA Ops:
  33.4 7.3 %dynamic-slice_multiply_fusion.11 = (f32[1,24,16,128]{3,2,1,0:T(8,128)}, f32[1,24,16,128]{3,2,1,0:T(8,128)S(1)}, f32[1,24,16,128]{3,2,1,0:T(8,128)}, f32[1,24,16...) fusion(f32[1,24,32,256]{3,2,1,0:T(8,128)} %param.10, s32[]{:T(128)S(6)} %select_n.61, ...), kind=kLoop, calls=%fused_computation.97 | loop fusion | flops 294912 | bytes 2359368 | tf_op jit(solution)/shard_map/mul | solution.py:125
  48.7 7.2 %multiply_reduce_fusion.1 = f32[24,16,128]{0,2,1:T(8,128)} fusion(f32[24,16,2,128,2]{0,4,3,2,1:T(2,128)} %bitcast.116, f32[16,2,128,2]{3,2,1,0:T(8,128)S(1)} %mul.540), kind=kLoop, calls=%fused_computation.1 | loop fusion | flops 344064 | bytes 1015808 | tf_op jit(solution)/shard_map/reduce_sum | solution.py:38
  57.4 17.7 %all-gather = f32[96,16,128]{2,1,0:T(8,128)S(1)} all-gather(f32[24,16,128]{2,1,0:T(8,128)S(1)} %copy.39), channel_id=2, replica_groups=mesh['grid'=4,'gx'=16,'gy'=8] {'grid'}, dimensions={0}, use_global_device_ids=true | all-gather | bytes 983040 | tf_op jit(solution)/shard_map/all_gather | solution.py:145
  95.0 4.5 %multiply_subtract_fusion = f32[32,256]{1,0:T(8,128)} fusion(f32[]{:T(128)} %bitcast.20, f32[]{:T(128)} %bitcast.17, f32[]{:T(128)} %bitcast.14, f32[]{:T(128)} %bitcast.11, f32[]{:T(128)} %bitcast.8, f32[]{:T(128)} %bitcast.5, pred[256]{0:T(512)(128)(4,1)S(1)} %iota_compare_fusion, pred[256]{0:T(512)(128)(4,1)S(1)} %iota_compare_fusion.1, ...), kind=kLoop, calls=%fused_computation.99 | loop fusion | flops 204800 | bytes 36056 | tf_op jit(solution)/shard_map/sub | solution.py:164
  100.4 9.0 %dynamic_update_slice.36 = f32[24,32,256]{2,1,0:T(8,128)} dynamic-update-slice(f32[24,32,256]{2,1,0:T(8,128)} %broadcast.563.clone, f32[24,16,128]{2,1,0:T(8,128)} %slice_bitcast_fusion.11, s32[]{:T(128)} %constant.55.clone.1, s32[]{:T(128)S(6)} %select_n.61, s32[]{:T(128)S(6)} %select_n.62) | dynamic-update-slice | bytes 393220 | tf_op jit(solution)/shard_map/dynamic_update_slice | solution.py:161
  116.5 9.0 %dynamic_update_slice.37 = f32[24,32,256]{2,1,0:T(8,128)} dynamic-update-slice(f32[24,32,256]{2,1,0:T(8,128)} %dynamic_update_slice.36, f32[24,16,128]{2,1,0:T(8,128)} %fusion.27, s32[]{:T(128)} %constant.55.clone.1, s32[]{:T(128)S(6)} %select_n.63, s32[]{:T(128)S(6)} %select_n.64) | dynamic-update-slice | bytes 393220 | tf_op jit(solution)/shard_map/dynamic_update_slice | solution.py:161
  127.3 8.4 %dynamic_update_slice.38 = f32[24,32,256]{2,1,0:T(8,128)} dynamic-update-slice(f32[24,32,256]{2,1,0:T(8,128)} %dynamic_update_slice.37, f32[24,16,128]{2,1,0:T(8,128)} %fusion.26, s32[]{:T(128)} %constant.55.clone.1, s32[]{:T(128)S(6)} %select_n.65, s32[]{:T(128)S(6)} %select_n.66) | dynamic-update-slice | bytes 393220 | tf_op jit(solution)/shard_map/dynamic_update_slice | solution.py:161
  137.7 9.0 %dynamic_update_slice.39 = f32[24,32,256]{2,1,0:T(8,128)} dynamic-update-slice(f32[24,32,256]{2,1,0:T(8,128)} %dynamic_update_slice.38, f32[24,16,128]{2,1,0:T(8,128)} %fusion.25, s32[]{:T(128)} %constant.55.clone.1, s32[]{:T(128)S(6)} %select_n.67, s32[]{:T(128)S(6)} %select_n.68) | dynamic-update-slice | bytes 393220 | tf_op jit(solution)/shard_map/dynamic_update_slice | solution.py:161
  148.5 9.0 %dynamic_update_slice.40 = f32[24,32,256]{2,1,0:T(8,128)} dynamic-update-slice(f32[24,32,256]{2,1,0:T(8,128)} %dynamic_update_slice.39, f32[24,16,128]{2,1,0:T(8,128)} %fusion.24, s32[]{:T(128)} %constant.55.clone.1, s32[]{:T(128)S(6)} %select_n.69, s32[]{:T(128)S(6)} %select_n.70) | dynamic-update-slice | bytes 393220 | tf_op jit(solution)/shard_map/dynamic_update_slice | solution.py:161
  158.8 9.0 %dynamic_update_slice.41 = f32[24,32,256]{2,1,0:T(8,128)} dynamic-update-slice(f32[24,32,256]{2,1,0:T(8,128)} %dynamic_update_slice.40, f32[24,16,128]{2,1,0:T(8,128)S(1)} %fusion.23, s32[]{:T(128)} %constant.55.clone.1, s32[]{:T(128)S(6)} %select_n.71, s32[]{:T(128)S(6)} %select_n.72) | dynamic-update-slice | bytes 393220 | tf_op jit(solution)/shard_map/dynamic_update_slice | solution.py:161
  167.8 13.7 %all-reduce.5.cloned.1.call-done = f32[3,24,16,128]{3,2,1,0:T(8,128)} async-done(((f32[3,24,16,128]{3,2,1,0:T(8,128)}), f32[3,24,16,128]{3,2,1,0:T(8,128)}) %all-reduce.5.cloned.1.call-update) | async-done | bytes 589840 | tf_op jit(solution)/shard_map/psum | solution.py:20
  184.2 3.3 broadcast_in_dim.17
  198.5 4.2 collective-permute-done.3
  202.9 11.8 %collective-permute-start.4 = (f32[1,24,34,1]{3,2,1,0:T(8,128)S(1)}, f32[1,24,34,1]{3,2,1,0:T(8,128)S(1)}, u32[]{:S(2)}, u32[]{:S(2)}) collective-permute-start(f32[1,24,34,1]{3,2,1,0:T(8,128)S(1)} %get-tuple-element.11), channel_id=1, source_target_pairs={{0,1},{1,2},{2,3},{3,4},{4,5},{5,6},{6,7},{8,9},{9,10},{10,11},{11... | collective-permute-start | bytes 9800 | tf_op jit(solution)/shard_map/ppermute | solution.py:30
  216.8 3.8 collective-permute-done.4
  220.7 23.0 %collective-permute-done.5 = f32[1,24,34,1]{3,2,1,0:T(8,128)S(1)} collective-permute-done((f32[1,24,34,1]{3,2,1,0:T(8,128)S(1)}, f32[1,24,34,1]{3,2,1,0:T(8,128)S(1)}, u32[]{:S(2)}, u32[]{:S(2)}) %collective-permute-start.5) | collective-permute-done | bytes 3296 | tf_op jit(solution)/shard_map/ppermute | solution.py:31
  244.5 5.0 %dynamic-slice_multiply_fusion.5 = (f32[1,24,16,128]{3,2,1,0:T(8,128)}, f32[1,24,16,128]{3,2,1,0:T(8,128)S(1)}, f32[1,24,16,128]{3,2,1,0:T(8,128)S(1)}, f32[1,24...) fusion(f32[1,24,32,256]{3,2,1,0:T(8,128)S(1)} %fusion.6, s32[]{:T(128)S(6)} %select_n.61, ...), kind=kLoop, calls=%fused_computation.90 | loop fusion | flops 294912 | bytes 2359368 | tf_op jit(solution)/shard_map/mul | solution.py:125
  254.9 7.2 %multiply_reduce_fusion = f32[24,16,128]{0,2,1:T(8,128)} fusion(f32[24,16,2,128,2]{0,4,3,2,1:T(2,128)} %bitcast.115, f32[16,2,128,2]{3,2,1,0:T(8,128)S(1)} %mul.540), kind=kLoop, calls=%fused_computation | loop fusion | flops 344064 | bytes 1015808 | tf_op jit(solution)/shard_map/reduce_sum | solution.py:38
  263.7 12.8 %all-gather.1 = f32[96,16,128]{2,1,0:T(8,128)S(1)} all-gather(f32[24,16,128]{2,1,0:T(8,128)S(1)} %copy.44), channel_id=3, replica_groups=mesh['grid'=4,'gx'=16,'gy'=8] {'grid'}, dimensions={0}, use_global_device_ids=true | all-gather | bytes 983040 | tf_op jit(solution)/shard_map/all_gather | solution.py:145
  277.5 3.3 collective-permute-start.6
  281.0 7.9 %dynamic_update_slice.42 = f32[24,32,256]{2,1,0:T(8,128)S(1)} dynamic-update-slice(f32[24,32,256]{2,1,0:T(8,128)S(1)} %broadcast.563, f32[24,16,128]{2,1,0:T(8,128)S(1)} %slice_bitcast_fusion.5, s32[]{:T(128)} %constant.55.clone.1, s32[]{:T(128)S(6)} %select_n.61, s32[]{:T(128)S(6)} %select_n.62) | dynamic-update-slice | bytes 393220 | tf_op jit(solution)/shard_map/dynamic_update_slice | solution.py:161
  291.1 7.9 %dynamic_update_slice.43 = f32[24,32,256]{2,1,0:T(8,128)S(1)} dynamic-update-slice(f32[24,32,256]{2,1,0:T(8,128)S(1)} %dynamic_update_slice.42, f32[24,16,128]{2,1,0:T(8,128)S(1)} %fusion.22, s32[]{:T(128)} %constant.55.clone.1, s32[]{:T(128)S(6)} %select_n.63, s32[]{:T(128)S(6)} %select_n.64) | dynamic-update-slice | bytes 393220 | tf_op jit(solution)/shard_map/dynamic_update_slice | solution.py:161
  299.1 7.7 %dynamic_update_slice.44 = f32[24,32,256]{2,1,0:T(8,128)S(1)} dynamic-update-slice(f32[24,32,256]{2,1,0:T(8,128)S(1)} %dynamic_update_slice.43, f32[24,16,128]{2,1,0:T(8,128)S(1)} %fusion.21, s32[]{:T(128)} %constant.55.clone.1, s32[]{:T(128)S(6)} %select_n.65, s32[]{:T(128)S(6)} %select_n.66) | dynamic-update-slice | bytes 393220 | tf_op jit(solution)/shard_map/dynamic_update_slice | solution.py:161
  307.0 7.9 %dynamic_update_slice.45 = f32[24,32,256]{2,1,0:T(8,128)S(1)} dynamic-update-slice(f32[24,32,256]{2,1,0:T(8,128)S(1)} %dynamic_update_slice.44, f32[24,16,128]{2,1,0:T(8,128)S(1)} %fusion.20, s32[]{:T(128)} %constant.55.clone.1, s32[]{:T(128)S(6)} %select_n.67, s32[]{:T(128)S(6)} %select_n.68) | dynamic-update-slice | bytes 393220 | tf_op jit(solution)/shard_map/dynamic_update_slice | solution.py:161
  315.0 7.9 %dynamic_update_slice.46 = f32[24,32,256]{2,1,0:T(8,128)S(1)} dynamic-update-slice(f32[24,32,256]{2,1,0:T(8,128)S(1)} %dynamic_update_slice.45, f32[24,16,128]{2,1,0:T(8,128)S(1)} %fusion.19, s32[]{:T(128)} %constant.55.clone.1, s32[]{:T(128)S(6)} %select_n.69, s32[]{:T(128)S(6)} %select_n.70) | dynamic-update-slice | bytes 393220 | tf_op jit(solution)/shard_map/dynamic_update_slice | solution.py:161
  323.1 7.9 %dynamic_update_slice.47 = f32[24,32,256]{2,1,0:T(8,128)S(1)} dynamic-update-slice(f32[24,32,256]{2,1,0:T(8,128)S(1)} %dynamic_update_slice.46, f32[24,16,128]{2,1,0:T(8,128)S(1)} %fusion.18, s32[]{:T(128)} %constant.55.clone.1, s32[]{:T(128)S(6)} %select_n.71, s32[]{:T(128)S(6)} %select_n.72) | dynamic-update-slice | bytes 393220 | tf_op jit(solution)/shard_map/dynamic_update_slice | solution.py:161
  331.0 20.2 %all-reduce.7.cloned.1.call-done = f32[3,24,16,128]{3,2,1,0:T(8,128)} async-done(((f32[3,24,16,128]{3,2,1,0:T(8,128)}), f32[3,24,16,128]{3,2,1,0:T(8,128)}) %all-reduce.7.cloned.1.call-update) | async-done | bytes 589840 | tf_op jit(solution)/shard_map/psum | solution.py:20
  353.9 3.3 broadcast_in_dim.20
  367.8 4.4 %collective-permute-done.9 = f32[1,24,1,256]{3,2,1,0:T(1,128)S(1)} collective-permute-done((f32[1,24,1,256]{3,2,1,0:T(1,128)S(1)}, f32[1,24,1,256]{3,2,1,0:T(1,128)S(1)}, u32[]{:S(2)}, u32[]{:S(2)}) %collective-permute-start.9) | collective-permute-done | bytes 24608 | tf_op jit(solution)/shard_map/ppermute | solution.py:31
  372.6 11.7 %collective-permute-start.10 = (f32[1,24,34,1]{3,2,1,0:T(8,128)S(1)}, f32[1,24,34,1]{3,2,1,0:T(8,128)S(1)}, u32[]{:S(2)}, u32[]{:S(2)}) collective-permute-start(f32[1,24,34,1]{3,2,1,0:T(8,128)S(1)} %get-tuple-element.9), channel_id=1, source_target_pairs={{0,1},{1,2},{2,3},{3,4},{4,5},{5,6},{6,7},{8,9},{9,10},{10,11},{11... | collective-permute-start | bytes 9800 | tf_op jit(solution)/shard_map/ppermute | solution.py:30
  386.2 4.0 collective-permute-done.10
  390.2 22.8 %collective-permute-done.11 = f32[1,24,34,1]{3,2,1,0:T(8,128)S(1)} collective-permute-done((f32[1,24,34,1]{3,2,1,0:T(8,128)S(1)}, f32[1,24,34,1]{3,2,1,0:T(8,128)S(1)}, u32[]{:S(2)}, u32[]{:S(2)}) %collective-permute-start.11) | collective-permute-done | bytes 3296 | tf_op jit(solution)/shard_map/ppermute | solution.py:31
  (140 shorter events, 85.9 us)
Async XLA Ops:
  6.5 37.4 %copy-start = (f32[1,24,32,256]{3,2,1,0:T(8,128)S(1)}, f32[1,24,32,256]{3,2,1,0:T(8,128)}, u32[]{:S(2)}) copy-start(f32[1,24,32,256]{3,2,1,0:T(8,128)} %param.10) | copy-start | bytes 2359300
  6.5 175.0 %all-reduce.5.cloned.1.call-start = ((), (), s32[]{:S(2)}) async-start(), calls=%async_computation | async-start | bytes 1179648 | tf_op jit(solution)/shard_map/psum | solution.py:20
  33.4 13.2 %copy-start.15 = (f32[1,32,256]{2,1,0:T(8,128)S(1)}, f32[1,32,256]{2,1,0:T(8,128)}, u32[]{:S(2)}) copy-start(f32[1,32,256]{2,1,0:T(8,128)} %param.15) | copy-start | bytes 98308
  41.6 70.7 %collective-permute-start.1 = (f32[3,24,16,128]{3,2,1,0:T(8,128)}, f32[3,24,16,128]{3,2,1,0:T(8,128)}, u32[]{:S(2)}, u32[]{:S(2)}) collective-permute-start(f32[3,24,16,128]{3,2,1,0:T(8,128)} %pad_maximum_fusion.20), channel_id=1, source_target_pairs={{0,8},{8,0},{16,24},{24,16},{32,40},{40,32},{48,56},{56,48},{64,72... | collective-permute-start | bytes 1769480 | tf_op jit(solution)/shard_map/ppermute | solution.py:15
  76.2 38.4 %collective-permute-start = (f32[3,24,16,128]{3,2,1,0:T(8,128)}, f32[3,24,16,128]{3,2,1,0:T(8,128)}, u32[]{:S(2)}, u32[]{:S(2)}) collective-permute-start(f32[3,24,16,128]{3,2,1,0:T(8,128)} %get-tuple-element.37), channel_id=1, source_target_pairs={{0,8},{8,0},{16,24},{24,16},{32,40},{40,32},{48,56},{56,48},{64,72... | collective-permute-start | bytes 1769480 | tf_op jit(solution)/shard_map/ppermute | solution.py:15
  114.5 236.7 %all-reduce.7.cloned.1.call-start = ((), (), s32[]{:S(2)}) async-start(), calls=%async_computation.1 | async-start | bytes 1179648 | tf_op jit(solution)/shard_map/psum | solution.py:20
  184.2 6.4 %copy-start.3 = (f32[32,256]{1,0:T(8,128)S(1)}, f32[32,256]{1,0:T(8,128)}, u32[]{:S(2)}) copy-start(f32[32,256]{1,0:T(8,128)} %multiply_subtract_fusion) | copy-start | bytes 98308
  187.5 4.8 %copy-start.5 = (f32[1,32,256]{2,1,0:T(8,128)S(1)}, f32[1,32,256]{2,1,0:T(8,128)}, u32[]{:S(2)}) copy-start(f32[1,32,256]{2,1,0:T(8,128)} %param.13) | copy-start | bytes 98308
  187.5 4.8 %copy-start.7 = (f32[1,32,256]{2,1,0:T(8,128)S(1)}, f32[1,32,256]{2,1,0:T(8,128)}, u32[]{:S(2)}) copy-start(f32[1,32,256]{2,1,0:T(8,128)} %param.14) | copy-start | bytes 98308
  187.5 4.8 %copy-start.9 = (f32[32,256]{1,0:T(8,128)S(1)}, f32[32,256]{1,0:T(8,128)}, u32[]{:S(2)}) copy-start(f32[32,256]{1,0:T(8,128)} %get-tuple-element.39) | copy-start | bytes 98308
  187.5 4.8 %copy-start.11 = (f32[32,256]{1,0:T(8,128)S(1)}, f32[32,256]{1,0:T(8,128)}, u32[]{:S(2)}) copy-start(f32[32,256]{1,0:T(8,128)} %get-tuple-element.40) | copy-start | bytes 98308
  187.5 4.8 %copy-start.13 = (f32[32,256]{1,0:T(8,128)S(1)}, f32[32,256]{1,0:T(8,128)}, u32[]{:S(2)}) copy-start(f32[32,256]{1,0:T(8,128)} %get-tuple-element.41) | copy-start | bytes 98308
  192.2 0.8 copy-start.16
  193.2 5.3 %collective-permute-start.2 = (f32[1,24,1,256]{3,2,1,0:T(1,128)S(1)}, f32[1,24,1,256]{3,2,1,0:T(1,128)S(1)}, u32[]{:S(2)}, u32[]{:S(2)}) collective-permute-start(f32[1,24,1,256]{3,2,1,0:T(1,128)S(1)} %get-tuple-element.27), channel_id=1, source_target_pairs={{0,8},{8,16},{16,24},{24,32},{32,40},{40,48},{48,56},{56,64},{64,7... | collective-permute-start | bytes 73736 | tf_op jit(solution)/shard_map/ppermute | solution.py:30
  195.9 6.7 %collective-permute-start.3 = (f32[1,24,1,256]{3,2,1,0:T(1,128)S(1)}, f32[1,24,1,256]{3,2,1,0:T(1,128)S(1)}, u32[]{:S(2)}, u32[]{:S(2)}) collective-permute-start(f32[1,24,1,256]{3,2,1,0:T(1,128)S(1)} %get-tuple-element.28), channel_id=1, source_target_pairs={{8,0},{16,8},{24,16},{32,24},{40,32},{48,40},{56,48},{64,56},{72,6... | collective-permute-start | bytes 73736 | tf_op jit(solution)/shard_map/ppermute | solution.py:31
  202.9 17.7 %collective-permute-start.4 = (f32[1,24,34,1]{3,2,1,0:T(8,128)S(1)}, f32[1,24,34,1]{3,2,1,0:T(8,128)S(1)}, u32[]{:S(2)}, u32[]{:S(2)}) collective-permute-start(f32[1,24,34,1]{3,2,1,0:T(8,128)S(1)} %get-tuple-element.11), channel_id=1, source_target_pairs={{0,1},{1,2},{2,3},{3,4},{4,5},{5,6},{6,7},{8,9},{9,10},{10,11},{11... | collective-permute-start | bytes 9800 | tf_op jit(solution)/shard_map/ppermute | solution.py:30
  214.7 28.9 %collective-permute-start.5 = (f32[1,24,34,1]{3,2,1,0:T(8,128)S(1)}, f32[1,24,34,1]{3,2,1,0:T(8,128)S(1)}, u32[]{:S(2)}, u32[]{:S(2)}) collective-permute-start(f32[1,24,34,1]{3,2,1,0:T(8,128)S(1)} %get-tuple-element.12), channel_id=1, source_target_pairs={{1,0},{2,1},{3,2},{4,3},{5,4},{6,5},{7,6},{9,8},{10,9},{11,10},{12... | collective-permute-start | bytes 9800 | tf_op jit(solution)/shard_map/ppermute | solution.py:31
  253.0 35.9 %collective-permute-start.7 = (f32[3,24,16,128]{3,2,1,0:T(8,128)}, f32[3,24,16,128]{3,2,1,0:T(8,128)}, u32[]{:S(2)}, u32[]{:S(2)}) collective-permute-start(f32[3,24,16,128]{3,2,1,0:T(8,128)} %pad_maximum_fusion.21), channel_id=1, source_target_pairs={{0,8},{8,0},{16,24},{24,16},{32,40},{40,32},{48,56},{56,48},{64,72... | collective-permute-start | bytes 1769480 | tf_op jit(solution)/shard_map/ppermute | solution.py:15
  262.1 26.8 %copy-start.1 = (f32[1,24,16,128]{3,2,1,0:T(8,128)S(1)}, f32[1,24,16,128]{3,2,1,0:T(8,128)}, u32[]{:S(2)}) copy-start(f32[1,24,16,128]{3,2,1,0:T(8,128)} %get-tuple-element.21) | copy-start | bytes 589828
  262.1 26.8 %copy-start.2 = (f32[1,24,16,128]{3,2,1,0:T(8,128)S(1)}, f32[1,24,16,128]{3,2,1,0:T(8,128)}, u32[]{:S(2)}) copy-start(f32[1,24,16,128]{3,2,1,0:T(8,128)} %get-tuple-element.25) | copy-start | bytes 589828
  277.5 13.4 %collective-permute-start.6 = (f32[3,24,16,128]{3,2,1,0:T(8,128)}, f32[3,24,16,128]{3,2,1,0:T(8,128)S(1)}, u32[]{:S(2)}, u32[]{:S(2)}) collective-permute-start(f32[3,24,16,128]{3,2,1,0:T(8,128)} %get-tuple-element.35), channel_id=1, source_target_pairs={{0,8},{8,0},{16,24},{24,16},{32,40},{40,32},{48,56},{56,48},{64,72... | collective-permute-start | bytes 1769480 | tf_op jit(solution)/shard_map/ppermute | solution.py:15
  353.9 6.4 %copy-start.4 = (f32[32,256]{1,0:T(8,128)S(1)}, f32[32,256]{1,0:T(8,128)}, u32[]{:S(2)}) copy-start(f32[32,256]{1,0:T(8,128)} %multiply_subtract_fusion) | copy-start | bytes 98308
  357.1 4.5 %copy-start.6 = (f32[1,32,256]{2,1,0:T(8,128)S(1)}, f32[1,32,256]{2,1,0:T(8,128)}, u32[]{:S(2)}) copy-start(f32[1,32,256]{2,1,0:T(8,128)} %param.13) | copy-start | bytes 98308
  357.1 4.5 %copy-start.8 = (f32[1,32,256]{2,1,0:T(8,128)S(1)}, f32[1,32,256]{2,1,0:T(8,128)}, u32[]{:S(2)}) copy-start(f32[1,32,256]{2,1,0:T(8,128)} %param.14) | copy-start | bytes 98308
  357.1 4.5 %copy-start.10 = (f32[32,256]{1,0:T(8,128)S(1)}, f32[32,256]{1,0:T(8,128)}, u32[]{:S(2)}) copy-start(f32[32,256]{1,0:T(8,128)} %get-tuple-element.39) | copy-start | bytes 98308
  357.1 4.5 %copy-start.12 = (f32[32,256]{1,0:T(8,128)S(1)}, f32[32,256]{1,0:T(8,128)}, u32[]{:S(2)}) copy-start(f32[32,256]{1,0:T(8,128)} %get-tuple-element.40) | copy-start | bytes 98308
  357.1 4.5 %copy-start.14 = (f32[32,256]{1,0:T(8,128)S(1)}, f32[32,256]{1,0:T(8,128)}, u32[]{:S(2)}) copy-start(f32[32,256]{1,0:T(8,128)} %get-tuple-element.41) | copy-start | bytes 98308
  361.6 0.8 copy-start.17
  362.5 5.3 %collective-permute-start.8 = (f32[1,24,1,256]{3,2,1,0:T(1,128)S(1)}, f32[1,24,1,256]{3,2,1,0:T(1,128)S(1)}, u32[]{:S(2)}, u32[]{:S(2)}) collective-permute-start(f32[1,24,1,256]{3,2,1,0:T(1,128)S(1)} %get-tuple-element.19), channel_id=1, source_target_pairs={{0,8},{8,16},{16,24},{24,32},{32,40},{40,48},{48,56},{56,64},{64,7... | collective-permute-start | bytes 73736 | tf_op jit(solution)/shard_map/ppermute | solution.py:30
  365.6 6.7 %collective-permute-start.9 = (f32[1,24,1,256]{3,2,1,0:T(1,128)S(1)}, f32[1,24,1,256]{3,2,1,0:T(1,128)S(1)}, u32[]{:S(2)}, u32[]{:S(2)}) collective-permute-start(f32[1,24,1,256]{3,2,1,0:T(1,128)S(1)} %get-tuple-element.20), channel_id=1, source_target_pairs={{8,0},{16,8},{24,16},{32,24},{40,32},{48,40},{56,48},{64,56},{72,6... | collective-permute-start | bytes 73736 | tf_op jit(solution)/shard_map/ppermute | solution.py:31
  372.6 17.6 %collective-permute-start.10 = (f32[1,24,34,1]{3,2,1,0:T(8,128)S(1)}, f32[1,24,34,1]{3,2,1,0:T(8,128)S(1)}, u32[]{:S(2)}, u32[]{:S(2)}) collective-permute-start(f32[1,24,34,1]{3,2,1,0:T(8,128)S(1)} %get-tuple-element.9), channel_id=1, source_target_pairs={{0,1},{1,2},{2,3},{3,4},{4,5},{5,6},{6,7},{8,9},{9,10},{10,11},{11... | collective-permute-start | bytes 9800 | tf_op jit(solution)/shard_map/ppermute | solution.py:30
  384.3 28.7 %collective-permute-start.11 = (f32[1,24,34,1]{3,2,1,0:T(8,128)S(1)}, f32[1,24,34,1]{3,2,1,0:T(8,128)S(1)}, u32[]{:S(2)}, u32[]{:S(2)}) collective-permute-start(f32[1,24,34,1]{3,2,1,0:T(8,128)S(1)} %get-tuple-element.10), channel_id=1, source_target_pairs={{1,0},{2,1},{3,2},{4,3},{5,4},{6,5},{7,6},{9,8},{10,9},{11,10},{12... | collective-permute-start | bytes 9800 | tf_op jit(solution)/shard_map/ppermute | solution.py:31
Sparse Core Ops, SparseCore 0:
  114.6 66.8 all-reduce.4
  291.1 60.0 all-reduce.6
where the time goes:
time: 424 us; the launch traced here: 422 us
  local copies, waits for them, and re-layouts  133 us (31%)
  waiting for transfers between devices  96.1 us (23%)
  other arithmetic  69.2 us (16%)
  starting transfers between devices  48.6 us (11%)
  between operations  44.1 us (10%)
  blocking collectives  30.5 us (7%)
    dynamic_update_slice x12, local copies, waits for them, and re-layouts, local(): lax.dynamic_update_slice(gathered, existing + pieces[slot], (anchor, tops...  101 us
    ppermute x4, waiting for transfers between devices, padded_2(): after = lax.ppermute(leading, axis, down)  54.4 us
    psum x2, waiting for transfers between devices, spread(): return lax.psum(block, axis)  33.9 us
    all_gather x2, blocking collectives, local(): lax.all_gather(child_block[None], 'grid', axis=0, tiled=True)[1:]  30.5 us
    ppermute x4, starting transfers between devices, padded_2(): before = lax.ppermute(last, axis, up)  29.3 us
    reduce_sum x2, other arithmetic, block_sums(): values.reshape(shape[:-2] + (shape[-2] // 2, 2, shape[-1] // 2, 2))  14.3 us
    mul x2, other arithmetic, local(): keep_here[slot]  12.3 us
    ppermute x4, starting transfers between devices, partner(): return lax.ppermute(value, axis, pairs)  10.5 us
  transfers between devices with their start and end apart: 14, of which 8 were waited for; matrix products, arithmetic and copies ran while one was open for 37% of the time, Pallas kernels for 0%

commit v1 on v0

--- a/solution.py
+++ b/solution.py
@@ -1,12 +1,24 @@
+import functools
 import jax
 import jax.numpy as jnp
 from jax import lax
 from jax.sharding import PartitionSpec as P
+from jax.lax import all_to_all, axis_size
 
 NCLS = 3
 LEV = 8
 STEPS = 2
 relaxation = 0.125
+
+
+def prepare_layers_all(page, device_axis, k_dim):
+    r1 = axis_size(device_axis)
+    high = jnp.stack(r1 * [page], axis=0)
+    carry = all_to_all(high, axis_name=device_axis, split_axis=0, concat_axis=0)
+    return jnp.concatenate(carry, axis=k_dim)
+
+
+_resolve_stacks_all = functools.partial(prepare_layers_all, device_axis="grid", k_dim=0)
 
 
 def partner(value, axis, distance):
@@ -142,7 +154,7 @@
                 for slot in range(slots)
             ]
         )
-        gathered_up = lax.all_gather(child_block[None], "grid", axis=0, tiled=True)[1:]
+        gathered_up = _resolve_stacks_all(child_block[None])[1:]
         up_keep = keep_here[:, None, None, None] * gathered_up
         up_send = (1.0 - keep_here)[:, None, None, None] * gathered_up
         up_cross, down_cross = partner((up_send, down_there), "gx", 0)

time: 424 us -> 494 us (1.17)
  waiting for transfers between devices: 96.1 us -> 181 us
  blocking collectives: 30.5 us -> 0 us
  starting transfers between devices: 48.6 us -> 56.7 us
    psum x2, waiting for transfers between devices: 33.9 us -> 117 us  [spread(): return lax.psum(block, axis)]
    all_gather x2 -> x0, blocking collectives: 30.5 us -> none  [local(): lax.all_gather(child_block[None], 'grid', axis=0, tiled=True)[1:]]
    all_to_all x0 -> x2, starting transfers between devices: none -> 9.11 us  [prepare_layers_all(): carry = all_to_all(high, axis_name=device_axis, split_axis=0, concat_axis=0)]
    ppermute x4, waiting for transfers between devices: 0.01 us -> 8.71 us  [partner(): return lax.ppermute(value, axis, pairs)]
    ppermute x4, waiting for transfers between devices: 54.4 us -> 49.4 us  [padded_2(): after = lax.ppermute(leading, axis, down)]
  transfers between devices with their start and end apart: 14 -> 16, of which waited for: 8 -> 9; matrix products, arithmetic and copies ran while one was open for 37% -> 17% of each run, Pallas kernels for 0% -> 0%
where the time goes in v1:
time: 494 us; the launch traced here: 492 us
  waiting for transfers between devices  181 us (37%)
  local copies, waits for them, and re-layouts  137 us (28%)
  other arithmetic  73.5 us (15%)
  starting transfers between devices  56.7 us (11%)
  between operations  43.9 us (9%)
    psum x2, waiting for transfers between devices, spread(): return lax.psum(block, axis)  117 us
    dynamic_update_slice x12, local copies, waits for them, and re-layouts, local(): lax.dynamic_update_slice(gathered, existing + pieces[slot], (anchor, tops...  101 us
    ppermute x4, waiting for transfers between devices, padded_2(): after = lax.ppermute(leading, axis, down)  49.4 us
    ppermute x4, starting transfers between devices, padded_2(): before = lax.ppermute(last, axis, up)  30.4 us
    reduce_sum x2, other arithmetic, block_sums(): values.reshape(shape[:-2] + (shape[-2] // 2, 2, shape[-1] // 2, 2))  14.3 us
    add x10, other arithmetic, local(): existing + pieces[slot]  12.4 us
    mul x2, other arithmetic, local(): keep_here[slot]  11 us
  transfers between devices with their start and end apart: 16, of which 9 were waited for; matrix products, arithmetic and copies ran while one was open for 17% of the time, Pallas kernels for 0%

profile of v1, /device:TPU:25, one launch (start us, length us, event | category | flops | bytes accessed | tf_op | source)
XLA Modules:
  0.0 491.8 jit_solution(3352885508497029369)
XLA Ops:
  33.3 6.6 %dynamic-slice_multiply_fusion.11 = (f32[1,24,16,128]{3,2,1,0:T(8,128)S(1)}, f32[1,24,16,128]{3,2,1,0:T(8,128)S(1)}, f32[1,24,16,128]{3,2,1,0:T(8,128)S(1)}, f32...) fusion(f32[1,24,32,256]{3,2,1,0:T(8,128)} %param.10, s32[]{:T(128)S(6)} %select_n.61, ...), kind=kLoop, calls=%fused_computation.91 | loop fusion | flops 294912 | bytes 2359368 | tf_op jit(solution)/shard_map/mul | solution.py:137
  47.9 7.2 %multiply_reduce_fusion.1 = f32[24,16,128]{0,2,1:T(8,128)} fusion(f32[24,16,2,128,2]{0,4,3,2,1:T(2,128)} %bitcast.127, f32[16,2,128,2]{3,2,1,0:T(8,128)S(1)} %mul.540), kind=kLoop, calls=%fused_computation.1 | loop fusion | flops 344064 | bytes 1015808 | tf_op jit(solution)/shard_map/reduce_sum | solution.py:50
  59.2 5.6 %all-to-all-start = ((f32[4,1,24,16,128]{4,3,2,1,0:T(8,128)}), f32[4,1,24,16,128]{4,3,2,1,0:T(8,128)}, u32[]{:S(2)}, u32[]{:S(2)}) async-start(f32[4,1,24,16,128]{4,3,2,1,0:T(8,128)} %stack.16), calls=%async_computation | async-start | bytes 1572864 | tf_op jit(solution)/shard_map/all_to_all | solution.py:17
  82.0 4.7 multiply_subtract_fusion
  97.2 58.3 %all-reduce.5.cloned.1.call-done = f32[3,24,16,128]{3,2,1,0:T(8,128)} async-done(((f32[3,24,16,128]{3,2,1,0:T(8,128)}), f32[3,24,16,128]{3,2,1,0:T(8,128)}) %all-reduce.5.cloned.1.call-update) | async-done | bytes 589840 | tf_op jit(solution)/shard_map/psum | solution.py:32
  159.9 3.2 broadcast_in_dim.12
  167.9 9.0 %dynamic_update_slice.36 = f32[24,32,256]{2,1,0:T(8,128)} dynamic-update-slice(f32[24,32,256]{2,1,0:T(8,128)} %broadcast.567.clone, f32[24,16,128]{2,1,0:T(8,128)} %slice_bitcast_fusion.13, s32[]{:T(128)} %constant.55.clone.1, s32[]{:T(128)S(6)} %select_n.61, s32[]{:T(128)S(6)} %select_n.62) | dynamic-update-slice | bytes 393220 | tf_op jit(solution)/shard_map/dynamic_update_slice | solution.py:173
  178.9 9.0 %dynamic_update_slice.37 = f32[24,32,256]{2,1,0:T(8,128)} dynamic-update-slice(f32[24,32,256]{2,1,0:T(8,128)} %dynamic_update_slice.36, f32[24,16,128]{2,1,0:T(8,128)} %fusion.31, s32[]{:T(128)} %constant.55.clone.1, s32[]{:T(128)S(6)} %select_n.63, s32[]{:T(128)S(6)} %select_n.64) | dynamic-update-slice | bytes 393220 | tf_op jit(solution)/shard_map/dynamic_update_slice | solution.py:173
  189.7 8.4 %dynamic_update_slice.38 = f32[24,32,256]{2,1,0:T(8,128)} dynamic-update-slice(f32[24,32,256]{2,1,0:T(8,128)} %dynamic_update_slice.37, f32[24,16,128]{2,1,0:T(8,128)} %fusion.30, s32[]{:T(128)} %constant.55.clone.1, s32[]{:T(128)S(6)} %select_n.65, s32[]{:T(128)S(6)} %select_n.66) | dynamic-update-slice | bytes 393220 | tf_op jit(solution)/shard_map/dynamic_update_slice | solution.py:173
  200.1 9.0 %dynamic_update_slice.39 = f32[24,32,256]{2,1,0:T(8,128)} dynamic-update-slice(f32[24,32,256]{2,1,0:T(8,128)} %dynamic_update_slice.38, f32[24,16,128]{2,1,0:T(8,128)} %fusion.29, s32[]{:T(128)} %constant.55.clone.1, s32[]{:T(128)S(6)} %select_n.67, s32[]{:T(128)S(6)} %select_n.68) | dynamic-update-slice | bytes 393220 | tf_op jit(solution)/shard_map/dynamic_update_slice | solution.py:173
  211.0 9.1 %dynamic_update_slice.40 = f32[24,32,256]{2,1,0:T(8,128)} dynamic-update-slice(f32[24,32,256]{2,1,0:T(8,128)} %dynamic_update_slice.39, f32[24,16,128]{2,1,0:T(8,128)} %fusion.28, s32[]{:T(128)} %constant.55.clone.1, s32[]{:T(128)S(6)} %select_n.69, s32[]{:T(128)S(6)} %select_n.70) | dynamic-update-slice | bytes 393220 | tf_op jit(solution)/shard_map/dynamic_update_slice | solution.py:173
  221.4 9.0 %dynamic_update_slice.41 = f32[24,32,256]{2,1,0:T(8,128)} dynamic-update-slice(f32[24,32,256]{2,1,0:T(8,128)} %dynamic_update_slice.40, f32[24,16,128]{2,1,0:T(8,128)S(1)} %fusion.27, s32[]{:T(128)} %constant.55.clone.1, s32[]{:T(128)S(6)} %select_n.71, s32[]{:T(128)S(6)} %select_n.72) | dynamic-update-slice | bytes 393220 | tf_op jit(solution)/shard_map/dynamic_update_slice | solution.py:173
  232.9 3.7 collective-permute-start.2
  239.0 4.3 collective-permute-done.3
  243.5 11.7 %collective-permute-start.4 = (f32[1,24,34,1]{3,1,2,0:T(8,128)S(1)}, f32[1,24,34,1]{3,1,2,0:T(8,128)S(1)}, u32[]{:S(2)}, u32[]{:S(2)}) collective-permute-start(f32[1,24,34,1]{3,1,2,0:T(8,128)S(1)} %get-tuple-element.15), channel_id=1, source_target_pairs={{0,1},{1,2},{2,3},{3,4},{4,5},{5,6},{6,7},{8,9},{9,10},{10,11},{11... | collective-permute-start | bytes 9800 | tf_op jit(solution)/shard_map/ppermute | solution.py:42
  260.4 20.6 %collective-permute-done.5 = f32[1,24,34,1]{3,1,2,0:T(8,128)S(1)} collective-permute-done((f32[1,24,34,1]{3,1,2,0:T(8,128)S(1)}, f32[1,24,34,1]{3,1,2,0:T(8,128)S(1)}, u32[]{:S(2)}, u32[]{:S(2)}) %collective-permute-start.5) | collective-permute-done | bytes 3296 | tf_op jit(solution)/shard_map/ppermute | solution.py:43
  285.0 7.1 %multiply_reduce_fusion = f32[24,16,128]{0,2,1:T(8,128)} fusion(f32[24,16,2,128,2]{0,4,3,2,1:T(2,128)} %bitcast.128, f32[16,2,128,2]{3,2,1,0:T(8,128)S(1)} %mul.540), kind=kLoop, calls=%fused_computation | loop fusion | flops 344064 | bytes 1015808 | tf_op jit(solution)/shard_map/reduce_sum | solution.py:50
  294.6 3.5 all-to-all-start.1
  298.2 4.4 dynamic-slice_multiply_fusion.5
  304.5 8.7 %collective-permute-done.7 = f32[3,24,16,128]{3,2,1,0:T(8,128)S(1)} collective-permute-done((f32[3,24,16,128]{3,2,1,0:T(8,128)S(1)}, f32[3,24,16,128]{3,2,1,0:T(8,128)S(1)}, u32[]{:S(2)}, u32[]{:S(2)}) %collective-permute-start.7) | collective-permute-done | bytes 589856 | tf_op jit(solution)/shard_map/ppermute | solution.py:27
  317.1 58.5 %all-reduce.7.cloned.1.call-done = f32[3,24,16,128]{3,2,1,0:T(8,128)} async-done(((f32[3,24,16,128]{3,2,1,0:T(8,128)}), f32[3,24,16,128]{3,2,1,0:T(8,128)}) %all-reduce.7.cloned.1.call-update) | async-done | bytes 589840 | tf_op jit(solution)/shard_map/psum | solution.py:32
  382.3 7.9 %dynamic_update_slice.42 = f32[24,32,256]{2,1,0:T(8,128)S(1)} dynamic-update-slice(f32[24,32,256]{2,1,0:T(8,128)S(1)} %broadcast.567, f32[24,16,128]{2,1,0:T(8,128)S(1)} %slice_bitcast_fusion.7, s32[]{:T(128)} %constant.55.clone.1, s32[]{:T(128)S(6)} %select_n.61, s32[]{:T(128)S(6)} %select_n.62) | dynamic-update-slice | bytes 393220 | tf_op jit(solution)/shard_map/dynamic_update_slice | solution.py:173
  391.3 7.9 %dynamic_update_slice.43 = f32[24,32,256]{2,1,0:T(8,128)S(1)} dynamic-update-slice(f32[24,32,256]{2,1,0:T(8,128)S(1)} %dynamic_update_slice.42, f32[24,16,128]{2,1,0:T(8,128)S(1)} %fusion.26, s32[]{:T(128)} %constant.55.clone.1, s32[]{:T(128)S(6)} %select_n.63, s32[]{:T(128)S(6)} %select_n.64) | dynamic-update-slice | bytes 393220 | tf_op jit(solution)/shard_map/dynamic_update_slice | solution.py:173
  399.3 7.7 %dynamic_update_slice.44 = f32[24,32,256]{2,1,0:T(8,128)S(1)} dynamic-update-slice(f32[24,32,256]{2,1,0:T(8,128)S(1)} %dynamic_update_slice.43, f32[24,16,128]{2,1,0:T(8,128)S(1)} %fusion.25, s32[]{:T(128)} %constant.55.clone.1, s32[]{:T(128)S(6)} %select_n.65, s32[]{:T(128)S(6)} %select_n.66) | dynamic-update-slice | bytes 393220 | tf_op jit(solution)/shard_map/dynamic_update_slice | solution.py:173
  408.1 7.9 %dynamic_update_slice.45 = f32[24,32,256]{2,1,0:T(8,128)S(1)} dynamic-update-slice(f32[24,32,256]{2,1,0:T(8,128)S(1)} %dynamic_update_slice.44, f32[24,16,128]{2,1,0:T(8,128)S(1)} %fusion.24, s32[]{:T(128)} %constant.55.clone.1, s32[]{:T(128)S(6)} %select_n.67, s32[]{:T(128)S(6)} %select_n.68) | dynamic-update-slice | bytes 393220 | tf_op jit(solution)/shard_map/dynamic_update_slice | solution.py:173
  416.1 7.9 %dynamic_update_slice.46 = f32[24,32,256]{2,1,0:T(8,128)S(1)} dynamic-update-slice(f32[24,32,256]{2,1,0:T(8,128)S(1)} %dynamic_update_slice.45, f32[24,16,128]{2,1,0:T(8,128)S(1)} %fusion.23, s32[]{:T(128)} %constant.55.clone.1, s32[]{:T(128)S(6)} %select_n.69, s32[]{:T(128)S(6)} %select_n.70) | dynamic-update-slice | bytes 393220 | tf_op jit(solution)/shard_map/dynamic_update_slice | solution.py:173
  425.1 7.9 %dynamic_update_slice.47 = f32[24,32,256]{2,1,0:T(8,128)S(1)} dynamic-update-slice(f32[24,32,256]{2,1,0:T(8,128)S(1)} %dynamic_update_slice.46, f32[24,16,128]{2,1,0:T(8,128)S(1)} %fusion.22, s32[]{:T(128)} %constant.55.clone.1, s32[]{:T(128)S(6)} %select_n.71, s32[]{:T(128)S(6)} %select_n.72) | dynamic-update-slice | bytes 393220 | tf_op jit(solution)/shard_map/dynamic_update_slice | solution.py:173
  435.3 3.2 collective-permute-start.8
  441.1 4.1 collective-permute-done.9
  445.4 11.8 %collective-permute-start.10 = (f32[1,24,34,1]{3,1,2,0:T(8,128)S(1)}, f32[1,24,34,1]{3,1,2,0:T(8,128)S(1)}, u32[]{:S(2)}, u32[]{:S(2)}) collective-permute-start(f32[1,24,34,1]{3,1,2,0:T(8,128)S(1)} %get-tuple-element.11), channel_id=1, source_target_pairs={{0,1},{1,2},{2,3},{3,4},{4,5},{5,6},{6,7},{8,9},{9,10},{10,11},{11... | collective-permute-start | bytes 9800 | tf_op jit(solution)/shard_map/ppermute | solution.py:42
  459.2 3.1 collective-permute-done.10
  462.3 20.4 %collective-permute-done.11 = f32[1,24,34,1]{3,1,2,0:T(8,128)S(1)} collective-permute-done((f32[1,24,34,1]{3,1,2,0:T(8,128)S(1)}, f32[1,24,34,1]{3,1,2,0:T(8,128)S(1)}, u32[]{:S(2)}, u32[]{:S(2)}) %collective-permute-start.11) | collective-permute-done | bytes 3296 | tf_op jit(solution)/shard_map/ppermute | solution.py:43
  (150 shorter events, 96.5 us)
Async XLA Ops:
  6.5 36.6 %copy-start = (f32[1,24,32,256]{3,2,1,0:T(8,128)S(1)}, f32[1,24,32,256]{3,2,1,0:T(8,128)}, u32[]{:S(2)}) copy-start(f32[1,24,32,256]{3,2,1,0:T(8,128)} %param.10) | copy-start | bytes 2359300
  33.2 12.6 %copy-start.12 = (f32[1,32,256]{2,1,0:T(8,128)S(1)}, f32[1,32,256]{2,1,0:T(8,128)}, u32[]{:S(2)}) copy-start(f32[1,32,256]{2,1,0:T(8,128)} %param.15) | copy-start | bytes 98308
  40.8 47.3 %collective-permute-start.1 = (f32[3,24,16,128]{3,2,1,0:T(8,128)}, f32[3,24,16,128]{3,2,1,0:T(8,128)}, u32[]{:S(2)}, u32[]{:S(2)}) collective-permute-start(f32[3,24,16,128]{3,2,1,0:T(8,128)} %pad_maximum_fusion.10), channel_id=1, source_target_pairs={{0,8},{8,0},{16,24},{24,16},{32,40},{40,32},{48,56},{56,48},{64,72... | collective-permute-start | bytes 1769480 | tf_op jit(solution)/shard_map/ppermute | solution.py:27
  59.2 31.0 %all-to-all-start = ((f32[4,1,24,16,128]{4,3,2,1,0:T(8,128)}), f32[4,1,24,16,128]{4,3,2,1,0:T(8,128)}, u32[]{:S(2)}, u32[]{:S(2)}) async-start(f32[4,1,24,16,128]{4,3,2,1,0:T(8,128)} %stack.16), calls=%async_computation | async-start | bytes 1572864 | tf_op jit(solution)/shard_map/all_to_all | solution.py:17
  64.8 90.7 %all-reduce.5.cloned.1.call-start = ((), (), s32[]{:S(2)}) async-start(), calls=%async_computation.2 | async-start | bytes 1179648 | tf_op jit(solution)/shard_map/psum | solution.py:32
  92.2 84.7 %collective-permute-start = (f32[3,24,16,128]{3,2,1,0:T(8,128)}, f32[3,24,16,128]{3,2,1,0:T(8,128)}, u32[]{:S(2)}, u32[]{:S(2)}) collective-permute-start(f32[3,24,16,128]{3,2,1,0:T(8,128)} %get-tuple-element.41), channel_id=1, source_target_pairs={{0,8},{8,0},{16,24},{24,16},{32,40},{40,32},{48,56},{56,48},{64,72... | collective-permute-start | bytes 1769480 | tf_op jit(solution)/shard_map/ppermute | solution.py:27
  211.0 21.0 %copy-start.2 = (f32[1,32,256]{2,1,0:T(8,128)S(1)}, f32[1,32,256]{2,1,0:T(8,128)}, u32[]{:S(2)}) copy-start(f32[1,32,256]{2,1,0:T(8,128)} %param.13) | copy-start | bytes 98308
  211.0 21.0 %copy-start.4 = (f32[1,32,256]{2,1,0:T(8,128)S(1)}, f32[1,32,256]{2,1,0:T(8,128)}, u32[]{:S(2)}) copy-start(f32[1,32,256]{2,1,0:T(8,128)} %param.14) | copy-start | bytes 98308
  211.0 21.0 %copy-start.6 = (f32[32,256]{1,0:T(8,128)S(1)}, f32[32,256]{1,0:T(8,128)}, u32[]{:S(2)}) copy-start(f32[32,256]{1,0:T(8,128)} %get-tuple-element.43) | copy-start | bytes 98308
  211.0 21.0 %copy-start.8 = (f32[32,256]{1,0:T(8,128)S(1)}, f32[32,256]{1,0:T(8,128)}, u32[]{:S(2)}) copy-start(f32[32,256]{1,0:T(8,128)} %get-tuple-element.44) | copy-start | bytes 98308
  211.0 21.0 %copy-start.10 = (f32[32,256]{1,0:T(8,128)S(1)}, f32[32,256]{1,0:T(8,128)}, u32[]{:S(2)}) copy-start(f32[32,256]{1,0:T(8,128)} %get-tuple-element.45) | copy-start | bytes 98308
  232.0 0.8 copy-start.13
  232.9 5.7 %collective-permute-start.2 = (f32[1,24,1,256]{3,1,2,0:T(8,128)S(1)}, f32[1,24,1,256]{3,1,2,0:T(8,128)S(1)}, u32[]{:S(2)}, u32[]{:S(2)}) collective-permute-start(f32[1,24,1,256]{3,1,2,0:T(8,128)S(1)} %copy.191), channel_id=1, source_target_pairs={{0,8},{8,16},{16,24},{24,32},{32,40},{40,48},{48,56},{56,64},{64,7... | collective-permute-start | bytes 73736 | tf_op jit(solution)/shard_map/ppermute | solution.py:42
  236.6 6.7 %collective-permute-start.3 = (f32[1,24,1,256]{3,1,2,0:T(8,128)S(1)}, f32[1,24,1,256]{3,1,2,0:T(8,128)S(1)}, u32[]{:S(2)}, u32[]{:S(2)}) collective-permute-start(f32[1,24,1,256]{3,1,2,0:T(8,128)S(1)} %copy.193), channel_id=1, source_target_pairs={{8,0},{16,8},{24,16},{32,24},{40,32},{48,40},{56,48},{64,56},{72,6... | collective-permute-start | bytes 73736 | tf_op jit(solution)/shard_map/ppermute | solution.py:43
  243.5 16.9 %collective-permute-start.4 = (f32[1,24,34,1]{3,1,2,0:T(8,128)S(1)}, f32[1,24,34,1]{3,1,2,0:T(8,128)S(1)}, u32[]{:S(2)}, u32[]{:S(2)}) collective-permute-start(f32[1,24,34,1]{3,1,2,0:T(8,128)S(1)} %get-tuple-element.15), channel_id=1, source_target_pairs={{0,1},{1,2},{2,3},{3,4},{4,5},{5,6},{6,7},{8,9},{9,10},{10,11},{11... | collective-permute-start | bytes 9800 | tf_op jit(solution)/shard_map/ppermute | solution.py:42
  255.2 25.7 %collective-permute-start.5 = (f32[1,24,34,1]{3,1,2,0:T(8,128)S(1)}, f32[1,24,34,1]{3,1,2,0:T(8,128)S(1)}, u32[]{:S(2)}, u32[]{:S(2)}) collective-permute-start(f32[1,24,34,1]{3,1,2,0:T(8,128)S(1)} %get-tuple-element.16), channel_id=1, source_target_pairs={{1,0},{2,1},{3,2},{4,3},{5,4},{6,5},{7,6},{9,8},{10,9},{11,10},{12... | collective-permute-start | bytes 9800 | tf_op jit(solution)/shard_map/ppermute | solution.py:43
  294.6 19.6 %all-to-all-start.1 = ((f32[4,1,24,16,128]{4,3,2,1,0:T(8,128)}), f32[4,1,24,16,128]{4,3,2,1,0:T(8,128)S(1)}, u32[]{:S(2)}, u32[]{:S(2)}) async-start(f32[4,1,24,16,128]{4,3,2,1,0:T(8,128)} %stack.20), calls=%async_computation.1 | async-start | bytes 1572864 | tf_op jit(solution)/shard_map/all_to_all | solution.py:17
  298.1 77.5 %all-reduce.7.cloned.1.call-start = ((), (), s32[]{:S(2)}) async-start(), calls=%async_computation.3 | async-start | bytes 1179648 | tf_op jit(solution)/shard_map/psum | solution.py:32
  302.6 10.6 %collective-permute-start.7 = (f32[3,24,16,128]{3,2,1,0:T(8,128)S(1)}, f32[3,24,16,128]{3,2,1,0:T(8,128)S(1)}, u32[]{:S(2)}, u32[]{:S(2)}) collective-permute-start(f32[3,24,16,128]{3,2,1,0:T(8,128)S(1)} %pad_maximum_fusion.11), channel_id=1, source_target_pairs={{0,8},{8,0},{16,24},{24,16},{32,40},{40,32},{48,56},{56,48},{64,72... | collective-permute-start | bytes 1769480 | tf_op jit(solution)/shard_map/ppermute | solution.py:27
  315.2 75.1 %collective-permute-start.6 = (f32[3,24,16,128]{3,2,1,0:T(8,128)}, f32[3,24,16,128]{3,2,1,0:T(8,128)}, u32[]{:S(2)}, u32[]{:S(2)}) collective-permute-start(f32[3,24,16,128]{3,2,1,0:T(8,128)} %get-tuple-element.31), channel_id=1, source_target_pairs={{0,8},{8,0},{16,24},{24,16},{32,40},{40,32},{48,56},{56,48},{64,72... | collective-permute-start | bytes 1769480 | tf_op jit(solution)/shard_map/ppermute | solution.py:27
  382.1 50.9 %copy-start.1 = (f32[32,256]{1,0:T(8,128)S(1)}, f32[32,256]{1,0:T(8,128)}, u32[]{:S(2)}) copy-start(f32[32,256]{1,0:T(8,128)} %subtract_bitcast_fusion) | copy-start | bytes 98308
  382.2 52.2 %copy-start.3 = (f32[1,32,256]{2,1,0:T(8,128)S(1)}, f32[1,32,256]{2,1,0:T(8,128)}, u32[]{:S(2)}) copy-start(f32[1,32,256]{2,1,0:T(8,128)} %param.13) | copy-start | bytes 98308
  382.3 52.2 %copy-start.5 = (f32[1,32,256]{2,1,0:T(8,128)S(1)}, f32[1,32,256]{2,1,0:T(8,128)}, u32[]{:S(2)}) copy-start(f32[1,32,256]{2,1,0:T(8,128)} %param.14) | copy-start | bytes 98308
  382.3 52.2 %copy-start.7 = (f32[32,256]{1,0:T(8,128)S(1)}, f32[32,256]{1,0:T(8,128)}, u32[]{:S(2)}) copy-start(f32[32,256]{1,0:T(8,128)} %get-tuple-element.43) | copy-start | bytes 98308
  382.3 52.2 %copy-start.9 = (f32[32,256]{1,0:T(8,128)S(1)}, f32[32,256]{1,0:T(8,128)}, u32[]{:S(2)}) copy-start(f32[32,256]{1,0:T(8,128)} %get-tuple-element.44) | copy-start | bytes 98308
  382.3 52.2 %copy-start.11 = (f32[32,256]{1,0:T(8,128)S(1)}, f32[32,256]{1,0:T(8,128)}, u32[]{:S(2)}) copy-start(f32[32,256]{1,0:T(8,128)} %get-tuple-element.45) | copy-start | bytes 98308
  434.4 0.8 copy-start.14
  435.3 5.3 %collective-permute-start.8 = (f32[1,24,1,256]{3,1,2,0:T(8,128)S(1)}, f32[1,24,1,256]{3,1,2,0:T(8,128)S(1)}, u32[]{:S(2)}, u32[]{:S(2)}) collective-permute-start(f32[1,24,1,256]{3,1,2,0:T(8,128)S(1)} %copy.204), channel_id=1, source_target_pairs={{0,8},{8,16},{16,24},{24,32},{32,40},{40,48},{48,56},{56,64},{64,7... | collective-permute-start | bytes 73736 | tf_op jit(solution)/shard_map/ppermute | solution.py:42
  438.6 6.7 %collective-permute-start.9 = (f32[1,24,1,256]{3,1,2,0:T(8,128)S(1)}, f32[1,24,1,256]{3,1,2,0:T(8,128)S(1)}, u32[]{:S(2)}, u32[]{:S(2)}) collective-permute-start(f32[1,24,1,256]{3,1,2,0:T(8,128)S(1)} %copy.206), channel_id=1, source_target_pairs={{8,0},{16,8},{24,16},{32,24},{40,32},{48,40},{56,48},{64,56},{72,6... | collective-permute-start | bytes 73736 | tf_op jit(solution)/shard_map/ppermute | solution.py:43
  445.4 16.9 %collective-permute-start.10 = (f32[1,24,34,1]{3,1,2,0:T(8,128)S(1)}, f32[1,24,34,1]{3,1,2,0:T(8,128)S(1)}, u32[]{:S(2)}, u32[]{:S(2)}) collective-permute-start(f32[1,24,34,1]{3,1,2,0:T(8,128)S(1)} %get-tuple-element.11), channel_id=1, source_target_pairs={{0,1},{1,2},{2,3},{3,4},{4,5},{5,6},{6,7},{8,9},{9,10},{10,11},{11... | collective-permute-start | bytes 9800 | tf_op jit(solution)/shard_map/ppermute | solution.py:42
  457.2 25.6 %collective-permute-start.11 = (f32[1,24,34,1]{3,1,2,0:T(8,128)S(1)}, f32[1,24,34,1]{3,1,2,0:T(8,128)S(1)}, u32[]{:S(2)}, u32[]{:S(2)}) collective-permute-start(f32[1,24,34,1]{3,1,2,0:T(8,128)S(1)} %get-tuple-element.12), channel_id=1, source_target_pairs={{1,0},{2,1},{3,2},{4,3},{5,4},{6,5},{7,6},{9,8},{10,9},{11,10},{12... | collective-permute-start | bytes 9800 | tf_op jit(solution)/shard_map/ppermute | solution.py:43
Sparse Core Ops, SparseCore 0:
  90.2 65.2 all-reduce.4
  314.3 61.2 all-reduce.6
